TPU v7x, 512 devices: a whole 4x8x8 slice. The times are simulated.
512 devices in a mesh: ctx: 64 (over x, z, core), head: 8 (over y).
Axes of the slice: x: 4, y: 8, z: 8, core: 2. Of those that a mesh axis runs over, the one named last changes fastest.
Arguments:
- queries: bfloat16 [12288, 4096], P('ctx', 'head'), may hold values from -6 to 6
- key_rows: bfloat16 [12288, 4096], P('ctx', 'head'), may hold values from -6 to 6
- value_rows: bfloat16 [12288, 4096], P('ctx', 'head'), may hold values from -120 to 120
- gate_rows: bfloat16 [12288, 4096], P('ctx', 'head'), may hold values from -8 to 8
- cotangent: bfloat16 [12288, 4096], P('ctx', 'head'), may hold values from -6 to 6
Outputs:
- grad_queries: bfloat16 [12288, 4096], P('ctx', 'head')
- grad_keys: bfloat16 [12288, 4096], P('ctx', 'head')
- grad_values: bfloat16 [12288, 4096], P('ctx', 'head')
- grad_gates: bfloat16 [12288, 4096], P('ctx', 'head')
All inputs are finite; a program needn't handle non-finite values.
Results may differ from a plain program's by a relative error of at most 0.0065.
Values sent between devices are 32-bit elements; how exact they have to be, the bound alone decides.
A program may use at most 64 MiB of HBM per device.

v0:
```python
import jax
import jax.numpy as jnp
from jax import lax
from jax.sharding import PartitionSpec as P

H = 32
DH = 128
EPSILON = 1e-06


def carried_in(part, axis, combine, identity, reverse):
    count = lax.axis_size(axis)
    place = lax.axis_index(axis)
    ahead = count - 1 - place if reverse else place
    gathered = lax.all_gather(part, axis)
    state = jnp.zeros_like(part) + jnp.asarray(identity, part.dtype)

    def one(step, state):
        source = count - 1 - step if reverse else step
        return combine(state, lax.dynamic_index_in_dim(gathered, source, 0, False))

    return lax.fori_loop(0, ahead, one, state)


def silu_slope(x):
    sig = jax.nn.sigmoid(x)
    return sig * (1.0 + x * (1.0 - sig))


def add_states(earlier, later):
    return earlier + later


def per_device(queries, key_rows, value_rows, gate_rows, cotangent):
    rows, width = queries.shape
    heads = width // DH
    full_width = H * DH
    q_float = queries.astype(jnp.float32)
    k_float = key_rows.astype(jnp.float32)
    lifted_q = jax.nn.silu(q_float).astype(jnp.bfloat16).reshape(rows, heads, DH)
    lifted_k = jax.nn.silu(k_float).astype(jnp.bfloat16).reshape(rows, heads, DH)
    values = value_rows.reshape(rows, heads, DH)
    causal = lax.broadcasted_iota(jnp.int32, (rows, rows), 0) >= lax.broadcasted_iota(
        jnp.int32, (rows, rows), 1
    )
    local_state = jnp.einsum("thd,the->hde", lifted_k, values, preferred_element_type=jnp.float32)
    prefix = carried_in(local_state, "ctx", add_states, jnp.zeros_like(local_state), False)
    scores = jnp.einsum("thd,shd->hts", lifted_q, lifted_k, preferred_element_type=jnp.float32)
    weights = jnp.where(causal[None], scores, 0.0).astype(jnp.bfloat16)
    prefix_low = prefix.astype(jnp.bfloat16)
    attended = jnp.einsum("hts,shd->thd", weights, values, preferred_element_type=jnp.float32)
    attended = attended + jnp.einsum(
        "thd,hde->the", lifted_q, prefix_low, preferred_element_type=jnp.float32
    )
    attended = attended.reshape(rows, width)
    sig = jax.nn.sigmoid(gate_rows.astype(jnp.float32))
    grad_out = cotangent.astype(jnp.float32)
    gated = grad_out * sig
    sumsq = lax.psum(jnp.sum(attended * attended, axis=1), "head")
    rms = jnp.sqrt(sumsq / full_width + EPSILON)[:, None]
    normed = attended / rms
    inner = lax.psum(jnp.sum(gated * normed, axis=1), "head")[:, None]
    grad_gates = (grad_out * normed * sig * (1.0 - sig)).astype(jnp.bfloat16)
    d_attn = (
        ((gated - normed * inner / full_width) / rms).astype(jnp.bfloat16).reshape(rows, heads, DH)
    )
    grad_local = jnp.einsum("thd,the->hde", lifted_q, d_attn, preferred_element_type=jnp.float32)
    suffix = carried_in(grad_local, "ctx", add_states, jnp.zeros_like(grad_local), True)
    suffix_low = suffix.astype(jnp.bfloat16)
    d_scores = jnp.einsum("the,she->hts", d_attn, values, preferred_element_type=jnp.float32)
    d_weights = jnp.where(causal[None], d_scores, 0.0).astype(jnp.bfloat16)
    grad_lq = jnp.einsum("hts,shd->thd", d_weights, lifted_k, preferred_element_type=jnp.float32)
    grad_lq = grad_lq + jnp.einsum(
        "the,hde->thd", d_attn, prefix_low, preferred_element_type=jnp.float32
    )
    grad_lk = jnp.einsum("hts,thd->shd", d_weights, lifted_q, preferred_element_type=jnp.float32)
    grad_lk = grad_lk + jnp.einsum(
        "she,hde->shd", values, suffix_low, preferred_element_type=jnp.float32
    )
    grad_v = jnp.einsum("hts,the->she", weights, d_attn, preferred_element_type=jnp.float32)
    grad_v = grad_v + jnp.einsum(
        "shd,hde->she", lifted_k, suffix_low, preferred_element_type=jnp.float32
    )
    grad_queries = (grad_lq.reshape(rows, width) * silu_slope(q_float)).astype(jnp.bfloat16)
    grad_keys = (grad_lk.reshape(rows, width) * silu_slope(k_float)).astype(jnp.bfloat16)
    grad_values = grad_v.reshape(rows, width).astype(jnp.bfloat16)
    return (grad_queries, grad_keys, grad_values, grad_gates)


def solution(mesh):
    in_specs = (
        P("ctx", "head"),
        P("ctx", "head"),
        P("ctx", "head"),
        P("ctx", "head"),
        P("ctx", "head"),
    )
    out_specs = (P("ctx", "head"), P("ctx", "head"), P("ctx", "head"), P("ctx", "head"))
    return jax.shard_map(
        per_device, mesh=mesh, in_specs=in_specs, out_specs=out_specs, check_vma=False
    )
```

profile of v0, /device:TPU:1, one launch (start us, length us, event | category | flops | bytes accessed | tf_op | source)
XLA Modules:
  0.0 394.5 jit_solution(7202193139114948521)
XLA Ops:
  7.2 1.3 fusion.26
  10.2 112.5 %all-gather.5.cloned.1.call-done = f32[256,128,128]{2,1,0:T(8,128)} async-done(((f32[4,128,128]{2,1,0:T(8,128)}), f32[256,128,128]{2,1,0:T(8,128)}) %all-gather.5.cloned.1.call-update) | async-done | bytes 16777232 | tf_op jit(solution)/shard_map/all_gather | solution.py:15
  122.7 1.0 while.22
  122.8 1.0 bitcast_add_fusion.4
  124.1 13.2 %psum.14 = f32[192]{0:T(256)S(1)} all-reduce(f32[192]{0:T(256)S(1)} %get-tuple-element.103), channel_id=1, replica_groups=mesh['ctx'=64,'head'=8] {'head'}, use_global_device_ids=true, to_apply=%region_3.4 | all-reduce | flops 192 | bytes 1536 | tf_op jit(solution)/shard_map/psum | solution.py:59
  137.3 1.3 multiply_reduce_fusion
  138.6 11.5 %psum.15 = f32[192]{0:T(256)S(1)} all-reduce(f32[192]{0:T(256)S(1)} %multiply_reduce_fusion), channel_id=1, replica_groups=mesh['ctx'=64,'head'=8] {'head'}, use_global_device_ids=true, to_apply=%region_5.6 | all-reduce | flops 192 | bytes 1536 | tf_op jit(solution)/shard_map/psum | solution.py:62
  150.0 2.0 fusion.9
  153.8 1.8 fusion.25
  156.3 165.3 %all-gather.7.cloned.1.call-done = f32[256,128,128]{2,1,0:T(8,128)} async-done(((f32[4,128,128]{2,1,0:T(8,128)}), f32[256,128,128]{2,1,0:T(8,128)}) %all-gather.7.cloned.1.call-update) | async-done | bytes 16777232 | tf_op jit(solution)/shard_map/all_gather | solution.py:15
  321.6 64.1 %while.23 = (s32[]{:T(128)}, f32[4,128,128]{2,1,0:T(8,128)S(1)}, s32[]{:T(128)}, f32[64,4,128,128]{3,2,1,0:T(8,128)}, s32[]{:T(128)}, /*index=5*/s32[]{:T(128)}, s32[]{:T(128)}, s32[]{:T(128)}) while((s32[]{:T(128)}, f32[4,128,128]{2,1,0:T(8,128)S(1)}, s32[]{:T(128)}, f32[64,4,128,128]{3,2,1,0:T(8,128)}, s32[]{:T(128)}, /*index=5*/s32[]{:T(128)}, ...), condition=%wide.region_7.8_spmd, body=%wide.region_6.7_spmd.sunk | while | flops 65542 | bytes 786575 | solution.py:22
  321.6 1.0 bitcast_add_fusion.5
  322.7 1.0 bitcast_add_fusion.5
  323.7 1.0 bitcast_add_fusion.5
  324.7 1.0 bitcast_add_fusion.5
  325.8 1.0 bitcast_add_fusion.5
  326.8 1.0 bitcast_add_fusion.5
  327.8 1.0 bitcast_add_fusion.5
  328.9 1.0 bitcast_add_fusion.5
  329.9 1.0 bitcast_add_fusion.5
  330.9 1.0 bitcast_add_fusion.5
  331.9 1.0 bitcast_add_fusion.5
  333.0 1.0 bitcast_add_fusion.5
  334.0 1.0 bitcast_add_fusion.5
  335.0 1.0 bitcast_add_fusion.5
  336.1 1.0 bitcast_add_fusion.5
  337.1 1.0 bitcast_add_fusion.5
  338.1 1.0 bitcast_add_fusion.5
  339.2 1.0 bitcast_add_fusion.5
  340.2 1.0 bitcast_add_fusion.5
  341.2 1.0 bitcast_add_fusion.5
  342.3 1.0 bitcast_add_fusion.5
  343.3 1.0 bitcast_add_fusion.5
  344.3 1.0 bitcast_add_fusion.5
  345.4 1.0 bitcast_add_fusion.5
  346.4 1.0 bitcast_add_fusion.5
  347.4 1.0 bitcast_add_fusion.5
  348.5 1.0 bitcast_add_fusion.5
  349.5 1.0 bitcast_add_fusion.5
  350.5 1.0 bitcast_add_fusion.5
  351.6 1.0 bitcast_add_fusion.5
  352.6 1.0 bitcast_add_fusion.5
  353.6 1.0 bitcast_add_fusion.5
  354.7 1.0 bitcast_add_fusion.5
  355.7 1.0 bitcast_add_fusion.5
  356.7 1.0 bitcast_add_fusion.5
  357.8 1.0 bitcast_add_fusion.5
  358.8 1.0 bitcast_add_fusion.5
  359.8 1.0 bitcast_add_fusion.5
  360.9 1.0 bitcast_add_fusion.5
  361.9 1.0 bitcast_add_fusion.5
  362.9 1.0 bitcast_add_fusion.5
  364.0 1.0 bitcast_add_fusion.5
  365.0 1.0 bitcast_add_fusion.5
  366.0 1.0 bitcast_add_fusion.5
  367.1 1.0 bitcast_add_fusion.5
  368.1 1.0 bitcast_add_fusion.5
  369.1 1.0 bitcast_add_fusion.5
  370.2 1.0 bitcast_add_fusion.5
  371.2 1.0 bitcast_add_fusion.5
  372.2 1.0 bitcast_add_fusion.5
  378.4 1.0 bitcast_add_fusion.5
  379.5 1.0 bitcast_add_fusion.5
  380.5 1.0 bitcast_add_fusion.5
  (35 shorter events, 15.5 us)
Async XLA Ops:
  7.2 1.4 copy-start
  7.2 379.6 %copy-start.1 = (bf16[192,512]{1,0:T(8,128)(2,1)S(1)}, bf16[192,512]{1,0:T(8,128)(2,1)}, u32[]{:S(2)}) copy-start(bf16[192,512]{1,0:T(8,128)(2,1)} %param.10) | copy-start | bytes 589828
  7.2 115.5 %all-gather.5.cloned.1.call-start = ((), (), s32[]{:S(2)}) async-start(), calls=%async_computation | async-start | bytes 17039360 | tf_op jit(solution)/shard_map/all_gather | solution.py:15
  9.6 312.0 %all-gather.7.cloned.1.call-start = ((), (), s32[]{:S(2)}) async-start(), calls=%async_computation.1 | async-start | bytes 17039360 | tf_op jit(solution)/shard_map/all_gather | solution.py:15
Sparse Core Ops, SparseCore 0:
  11.4 111.3 all-gather.4
  153.1 168.3 all-gather.6
where the time goes:
time: 397 us; the launch traced here: 394 us
  waiting for transfers between devices  278 us (70%)
  other arithmetic  70.8 us (18%)
  blocking collectives  24.7 us (6%)
  between operations  14.2 us (4%)
  matrix products  4.67 us (1%)
    all_gather x2, waiting for transfers between devices, carried_in(): gathered = lax.all_gather(part, axis)  278 us
    add x63, other arithmetic, add_states(): return earlier + later  63.7 us
    psum x1, blocking collectives, per_device(): sumsq = lax.psum(jnp.sum(attended * attended, axis=1), 'head')  13.2 us
    psum x1, blocking collectives, per_device(): inner = lax.psum(jnp.sum(gated * normed, axis=1), 'head')[:, None]  11.5 us
  transfers between devices with their start and end apart: 2, of which 2 were waited for; matrix products, arithmetic and copies ran while one was open for 1% of the time, Pallas kernels for 0%

commit v1 on v0

--- a/solution.py
+++ b/solution.py
@@ -56,7 +56,7 @@
     sig = jax.nn.sigmoid(gate_rows.astype(jnp.float32))
     grad_out = cotangent.astype(jnp.float32)
     gated = grad_out * sig
-    sumsq = lax.psum(jnp.sum(attended * attended, axis=1), "head")
+    sumsq = jnp.sum(lax.all_gather(jnp.sum(attended * attended, axis=1), "head"), axis=0)
     rms = jnp.sqrt(sumsq / full_width + EPSILON)[:, None]
     normed = attended / rms
     inner = lax.psum(jnp.sum(gated * normed, axis=1), "head")[:, None]

time: 397 us -> 397 us (level)
    unnamed x0 -> x1, blocking collectives: none -> 13.4 us
    psum x1 -> x0, blocking collectives: 13.2 us -> none  [per_device(): sumsq = lax.psum(jnp.sum(attended * attended, axis=1), 'head')]
where the time goes in v1:
time: 397 us; the launch traced here: 395 us
  waiting for transfers between devices  276 us (70%)
  other arithmetic  70.9 us (18%)
  blocking collectives  24.9 us (6%)
  between operations  14.8 us (4%)
  matrix products  4.65 us (1%)
    all_gather x2, waiting for transfers between devices, carried_in(): gathered = lax.all_gather(part, axis)  276 us
    add x63, other arithmetic, add_states(): return earlier + later  63.7 us
    unnamed x1, blocking collectives  13.4 us
    psum x1, blocking collectives, per_device(): inner = lax.psum(jnp.sum(gated * normed, axis=1), 'head')[:, None]  11.5 us
  transfers between devices with their start and end apart: 2, of which 2 were waited for; matrix products, arithmetic and copies ran while one was open for 1% of the time, Pallas kernels for 0%

profile of v1, /device:TPU:1, one launch (start us, length us, event | category | flops | bytes accessed | tf_op | source)
XLA Modules:
  0.0 395.1 jit_solution(17875943315351818516)
XLA Ops:
  7.2 1.3 fusion.26
  9.6 1.3 dynamic-slice
  12.1 110.6 %all-gather.6.cloned.1.call-done = f32[256,128,128]{2,1,0:T(8,128)} async-done(((f32[4,128,128]{2,1,0:T(8,128)}), f32[256,128,128]{2,1,0:T(8,128)}) %all-gather.6.cloned.1.call-update) | async-done | bytes 16777232 | tf_op jit(solution)/shard_map/all_gather | solution.py:15
  122.7 1.0 while.22
  122.8 1.0 bitcast_add_fusion.4
  124.4 13.4 %all-reduce = f32[1536]{0:T(1024)S(1)} all-reduce(f32[1536]{0:T(1024)S(1)} %dynamic-update-slice), channel_id=3, replica_groups=mesh['ctx'=64,'head'=8] {'head'}, use_global_device_ids=true, to_apply=%add | all-reduce | flops 1536 | bytes 12288
  137.9 1.3 multiply_reduce_fusion
  139.2 11.5 %psum.7 = f32[192]{0:T(256)S(1)} all-reduce(f32[192]{0:T(256)S(1)} %multiply_reduce_fusion), channel_id=1, replica_groups=mesh['ctx'=64,'head'=8] {'head'}, use_global_device_ids=true, to_apply=%region_5.6 | all-reduce | flops 192 | bytes 1536 | tf_op jit(solution)/shard_map/psum | solution.py:62
  150.7 2.0 fusion.9
  154.4 1.8 fusion.25
  156.9 165.3 %all-gather.8.cloned.1.call-done = f32[256,128,128]{2,1,0:T(8,128)} async-done(((f32[4,128,128]{2,1,0:T(8,128)}), f32[256,128,128]{2,1,0:T(8,128)}) %all-gather.8.cloned.1.call-update) | async-done | bytes 16777232 | tf_op jit(solution)/shard_map/all_gather | solution.py:15
  322.2 64.1 %while.23 = (s32[]{:T(128)}, f32[4,128,128]{2,1,0:T(8,128)S(1)}, s32[]{:T(128)}, f32[64,4,128,128]{3,2,1,0:T(8,128)}, s32[]{:T(128)}, /*index=5*/s32[]{:T(128)}, s32[]{:T(128)}, s32[]{:T(128)}) while((s32[]{:T(128)}, f32[4,128,128]{2,1,0:T(8,128)S(1)}, s32[]{:T(128)}, f32[64,4,128,128]{3,2,1,0:T(8,128)}, s32[]{:T(128)}, /*index=5*/s32[]{:T(128)}, ...), condition=%wide.region_7.8_spmd, body=%wide.region_6.7_spmd.sunk | while | flops 65542 | bytes 786575 | solution.py:22
  322.3 1.0 bitcast_add_fusion.5
  323.3 1.0 bitcast_add_fusion.5
  324.3 1.0 bitcast_add_fusion.5
  325.4 1.0 bitcast_add_fusion.5
  326.4 1.0 bitcast_add_fusion.5
  327.4 1.0 bitcast_add_fusion.5
  328.5 1.0 bitcast_add_fusion.5
  329.5 1.0 bitcast_add_fusion.5
  330.5 1.0 bitcast_add_fusion.5
  331.6 1.0 bitcast_add_fusion.5
  332.6 1.0 bitcast_add_fusion.5
  333.6 1.0 bitcast_add_fusion.5
  334.7 1.0 bitcast_add_fusion.5
  335.7 1.0 bitcast_add_fusion.5
  336.7 1.0 bitcast_add_fusion.5
  337.8 1.0 bitcast_add_fusion.5
  338.8 1.0 bitcast_add_fusion.5
  339.8 1.0 bitcast_add_fusion.5
  340.9 1.0 bitcast_add_fusion.5
  341.9 1.0 bitcast_add_fusion.5
  342.9 1.0 bitcast_add_fusion.5
  344.0 1.0 bitcast_add_fusion.5
  345.0 1.0 bitcast_add_fusion.5
  346.0 1.0 bitcast_add_fusion.5
  347.1 1.0 bitcast_add_fusion.5
  348.1 1.0 bitcast_add_fusion.5
  349.1 1.0 bitcast_add_fusion.5
  350.2 1.0 bitcast_add_fusion.5
  351.2 1.0 bitcast_add_fusion.5
  352.2 1.0 bitcast_add_fusion.5
  353.3 1.0 bitcast_add_fusion.5
  354.3 1.0 bitcast_add_fusion.5
  355.3 1.0 bitcast_add_fusion.5
  356.4 1.0 bitcast_add_fusion.5
  357.4 1.0 bitcast_add_fusion.5
  358.4 1.0 bitcast_add_fusion.5
  359.5 1.0 bitcast_add_fusion.5
  360.5 1.0 bitcast_add_fusion.5
  361.5 1.0 bitcast_add_fusion.5
  362.6 1.0 bitcast_add_fusion.5
  363.6 1.0 bitcast_add_fusion.5
  364.6 1.0 bitcast_add_fusion.5
  365.7 1.0 bitcast_add_fusion.5
  366.7 1.0 bitcast_add_fusion.5
  367.7 1.0 bitcast_add_fusion.5
  368.8 1.0 bitcast_add_fusion.5
  369.8 1.0 bitcast_add_fusion.5
  370.8 1.0 bitcast_add_fusion.5
  371.9 1.0 bitcast_add_fusion.5
  379.1 1.0 bitcast_add_fusion.5
  380.1 1.0 bitcast_add_fusion.5
  381.2 1.0 bitcast_add_fusion.5
  (40 shorter events, 16.9 us)
Async XLA Ops:
  7.2 1.4 copy-start
  7.2 380.3 %copy-start.1 = (bf16[192,512]{1,0:T(8,128)(2,1)S(1)}, bf16[192,512]{1,0:T(8,128)(2,1)}, u32[]{:S(2)}) copy-start(bf16[192,512]{1,0:T(8,128)(2,1)} %param.10) | copy-start | bytes 589828
  7.2 115.5 %all-gather.6.cloned.1.call-start = ((), (), s32[]{:S(2)}) async-start(), calls=%async_computation | async-start | bytes 17039360 | tf_op jit(solution)/shard_map/all_gather | solution.py:15
  9.6 312.6 %all-gather.8.cloned.1.call-start = ((), (), s32[]{:S(2)}) async-start(), calls=%async_computation.1 | async-start | bytes 17039360 | tf_op jit(solution)/shard_map/all_gather | solution.py:15
Sparse Core Ops, SparseCore 0:
  11.4 111.3 all-gather.5
  153.8 168.4 all-gather.7
